TPU v7x, 32 devices: a whole 2x2x4 slice. The times are simulated.
32 devices in a mesh: groups: 2 (over x), replica: 4 (over z), tensor: 4 (over y, core).
Axes of the slice: x: 2, y: 2, z: 4, core: 2. Of those that a mesh axis runs over, the one named last changes fastest.
Arguments:
- queries: bfloat16 [4096, 4096], P(('groups', 'replica'), 'tensor'), parts along dimension 0, may hold values from -8 to 8
- new_kv: bfloat16 [4096, 2, 512], P(('groups', 'replica'), None, 'tensor'), parts along dimension 0, may hold values from -6 to 6, as said below
- cache_kv: bfloat16 [16, 4096, 2, 512], P(('groups', 'replica'), None, None, 'tensor'), parts along dimension 0, may hold values from -6 to 6, as said below
- stored: int32 [8, 2], P('groups'), parts along dimension 0, may hold values from 0 to 3, as said below
- haystack_ids: int32 [64, 1], P(('groups', 'replica')), parts along dimension 0, may hold values from 0 to 3; in each aligned block of 8 rows (0 to 7, 8 to 15, ...) at most 2 rows name the same one
- token_counts: int32 [8, 8], P(('groups', 'replica')), parts along dimension 0, may hold values from 1 to 64, 384 in all within a row
- out_weight: bfloat16 [4096, 8192], P('tensor'), may hold values from -0.75 to 0.75
Outputs:
- answer: bfloat16 [4096, 8192], P(('groups', 'replica'), 'tensor'), parts along dimension 0
There are 2 independent parts, one for each index of `groups`. A program takes and returns all parts, laid end to end along the dimension named above; an argument that names none is the same for every part. Nothing has to cross between parts.
Inputs may be any that keep to these rules, and one draw needn't show every extreme that they name: `stored`: every haystack lies in slot 0 of exactly one replica index and in slot 1 of exactly one other. `haystack_ids`: among the 8 questions of one replica index no haystack is named more than 2 times; some haystack is named exactly 2 times. `token_counts`: the counts of one replica index sum to 384 and the largest is 64. `cache_kv`: slots holding the same haystack hold equal values; the cache heads serving one kv head are equal. `new_kv`: the cache heads serving one kv head are equal.
All inputs are finite; a program needn't handle non-finite values.
Results may differ from a plain program's by a relative error of at most 0.0053.
Values may be sent and summed in bfloat16 or wider, within the bound.
No kernel may reach another device: no remote copies, remote signals or barrier semaphores. Data moves between devices by JAX's collectives and lax.ppermute only.
A program may use at most 128 MiB of HBM per device.

v0:
```python
import math

import jax
import jax.numpy as jnp
from jax import lax
from jax.sharding import PartitionSpec as P

CAP = 2


def attend_block(query_block, own_block, cache_slot):
    capacity, qlength, width = query_block.shape
    head_size = cache_slot.shape[-1]
    context = cache_slot.shape[0]
    heads = width // head_size
    scale = 1.0 / math.sqrt(head_size)
    query = query_block.reshape(capacity, qlength, heads, head_size)
    far = (
        lax.dot_general(
            query.reshape(-1, head_size),
            cache_slot[:, 0],
            (((1,), (1,)), ((), ())),
            preferred_element_type=jnp.float32,
        )
        * scale
    )
    far = far.reshape(capacity, qlength, heads, context)
    near = (
        jnp.einsum("cthd,cud->cthu", query, own_block[:, :, 0], preferred_element_type=jnp.float32)
        * scale
    )
    causal = jnp.arange(qlength)[:, None] >= jnp.arange(qlength)[None, :]
    near = jnp.where(causal[None, :, None, :], near, -jnp.inf)
    top = jnp.maximum(jnp.max(far, axis=-1), jnp.max(near, axis=-1))
    far_exp = jnp.exp(far - top[..., None])
    near_exp = jnp.exp(near - top[..., None])
    total = jnp.sum(far_exp, axis=-1) + jnp.sum(near_exp, axis=-1)
    far_weight = far_exp.astype(jnp.bfloat16).reshape(-1, context)
    near_weight = near_exp.astype(jnp.bfloat16)
    mixed = jnp.dot(far_weight, cache_slot[:, 1], preferred_element_type=jnp.float32)
    mixed = mixed.reshape(capacity, qlength, heads, head_size)
    mixed = mixed + jnp.einsum(
        "cthu,cud->cthd", near_weight, own_block[:, :, 1], preferred_element_type=jnp.float32
    )
    result = mixed / total[..., None]
    return result.astype(jnp.bfloat16).reshape(capacity, qlength, width)


def on_device(queries, new_kv, cache_kv, stored, haystack_ids, token_counts, out_weight):
    replicas = lax.axis_size("replica")
    slots = stored.shape[1]
    head_size = cache_kv.shape[-1]
    questions = haystack_ids.shape[0]
    qlength = queries.shape[0] // questions
    width = queries.shape[1]
    capacity = CAP
    wanted_ids = haystack_ids[:, 0]
    order = jnp.arange(questions, dtype=jnp.int32)
    before = order[None, :] < order[:, None]
    chosen = jnp.zeros((questions,), jnp.int32)
    matches = stored[None, :, :] == wanted_ids[:, None, None]
    slot_place = jnp.arange(slots, dtype=jnp.int32)[None, None, :]
    target = matches & (slot_place == chosen[:, None, None])
    replica_codes = jnp.broadcast_to(
        jnp.arange(replicas, dtype=jnp.int32)[None, :, None], (1, replicas, slots)
    )
    dest = jnp.sum(jnp.where(target, replica_codes, 0), axis=(1, 2))
    same_dest = (dest[None, :] == dest[:, None]) & before
    position = dest * capacity + jnp.sum(same_dest.astype(jnp.int32), axis=1)
    buffers = replicas * capacity
    send_query = jnp.zeros((buffers, qlength, width), jnp.bfloat16)
    send_query = send_query.at[position].set(queries.reshape(questions, qlength, width))
    send_own = jnp.zeros((buffers, qlength, 2, head_size), jnp.bfloat16)
    send_own = send_own.at[position].set(new_kv.reshape(questions, qlength, 2, head_size))
    slot_code = (chosen + 1).astype(jnp.bfloat16)
    send_code = jnp.zeros((buffers,), jnp.bfloat16).at[position].set(slot_code)
    got_query, got_own, got_code = (
        lax.all_to_all(
            send_query.reshape(replicas, capacity * qlength, width),
            "replica",
            split_axis=0,
            concat_axis=0,
            tiled=True,
        ),
        lax.all_to_all(
            send_own.reshape(replicas, capacity * qlength, 2, head_size),
            "replica",
            split_axis=0,
            concat_axis=0,
            tiled=True,
        ),
        lax.all_to_all(
            send_code.reshape(replicas, capacity),
            "replica",
            split_axis=0,
            concat_axis=0,
            tiled=True,
        ),
    )
    query_rows = got_query.reshape(buffers, 1, qlength, width)
    own_rows = got_own.reshape(buffers, 1, qlength, 2, head_size)
    codes = got_code.reshape(buffers).astype(jnp.float32)
    busy_rows = codes > 0.5
    slot_of = (codes > 1.5).astype(jnp.int32)

    def run_question(items):
        query_block, own_block, busy, slot_index = items
        cache_slot = lax.dynamic_index_in_dim(cache_kv, slot_index, 0, keepdims=False)
        return lax.cond(
            busy,
            lambda: attend_block(query_block, own_block, cache_slot),
            lambda: jnp.zeros((1, qlength, width), jnp.bfloat16),
        )

    results = lax.map(run_question, (query_rows, own_rows, busy_rows, slot_of))
    returned = lax.all_to_all(
        results.reshape(replicas, capacity * qlength, width),
        "replica",
        split_axis=0,
        concat_axis=0,
        tiled=True,
    )
    returned = returned.reshape(buffers, qlength, width)[position]
    counts = token_counts[0]
    used = jnp.arange(qlength, dtype=jnp.int32)[None, :] < counts[:, None]
    attended = jnp.where(used[..., None], returned, jnp.zeros_like(returned))
    attended = attended.reshape(questions * qlength, width)
    summed = lax.psum_scatter(
        lax.dot_general(
            out_weight, attended, (((0,), (1,)), ((), ())), preferred_element_type=jnp.float32
        ),
        "tensor",
        scatter_dimension=0,
        tiled=True,
    )
    return summed.T.astype(jnp.bfloat16)


def solution(mesh):
    in_specs = (
        P(("groups", "replica"), "tensor"),
        P(("groups", "replica"), None, "tensor"),
        P(("groups", "replica"), None, None, "tensor"),
        P("groups", None),
        P(("groups", "replica"), None),
        P(("groups", "replica"), None),
        P("tensor", None),
    )
    out_specs = P(("groups", "replica"), "tensor")
    return jax.shard_map(
        on_device, mesh=mesh, in_specs=in_specs, out_specs=out_specs, check_vma=False
    )
```

profile of v0, /device:TPU:0, one launch (start us, length us, event | category | flops | bytes accessed | tf_op | source)
XLA Modules:
  0.0 351.1 jit_solution(13047620546977627329)
XLA Ops:
  8.8 6.3 %all-to-all-start = ((bf16[4,1,2]{2,1,0:T(2,128)(2,1)}), bf16[4,1,2]{2,1,0:T(2,128)(2,1)S(1)}, u32[]{:S(2)}, u32[]{:S(2)}) async-start(bf16[4,1,2]{2,1,0:T(2,128)(2,1)} %all_to_all.20), calls=%async_computation | async-start | bytes 4096 | tf_op jit(solution)/shard_map/all_to_all | solution.py:92
  17.8 2.8 all-to-all-done
  20.6 3.4 all-to-all-start.2
  25.2 3.3 scatter_fusion
  28.4 3.6 %all-to-all-done.2 = bf16[4,128,2,128]{3,1,2,0:T(8,128)(2,1)S(1)} async-done(((bf16[4,128,2,128]{3,1,2,0:T(8,128)(2,1)}), bf16[4,128,2,128]{3,1,2,0:T(8,128)(2,1)S(1)}, u32[]{:S(2)}, u32[]{:S(2)}) %all-to-all-start.2) | async-done | bytes 262176 | tf_op jit(solution)/shard_map/all_to_all | solution.py:85
  32.1 4.2 %all-to-all-start.1 = ((bf16[4,128,1024]{2,1,0:T(8,128)(2,1)}), bf16[4,128,1024]{2,1,0:T(8,128)(2,1)}, u32[]{:S(2)}, u32[]{:S(2)}) async-start(bf16[4,128,1024]{2,1,0:T(8,128)(2,1)} %bitcast.17), calls=%async_computation.1 | async-start | bytes 2097152 | tf_op jit(solution)/shard_map/all_to_all | solution.py:78
  36.3 4.7 %copy.37 = bf16[2,4096,2,128]{3,1,2,0:T(8,128)(2,1)} copy(bf16[2,4096,2,128]{3,2,1,0:T(2,128)(2,1)} %param.13) | data formatting | bytes 8388608 | tf_op jit(solution)/shard_map/while | solution.py:115
  41.2 18.2 %all-to-all-done.1 = bf16[4,128,1024]{2,1,0:T(8,128)(2,1)} async-done(((bf16[4,128,1024]{2,1,0:T(8,128)(2,1)}), bf16[4,128,1024]{2,1,0:T(8,128)(2,1)}, u32[]{:S(2)}, u32[]{:S(2)}) %all-to-all-start.1) | async-done | bytes 1048608 | tf_op jit(solution)/shard_map/all_to_all | solution.py:78
  59.4 111.8 %while.10 = (s32[]{:T(128)}, bf16[8,1,64,1024]{3,2,1,0:T(8,128)(2,1)}, pred[8]{0:T(512)(128)(4,1)S(1)}, bf16[8,1,64,1024]{3,2,1,0:T(8,128)(2,1)}, s32[8]{0:T(128...) while((s32[]{:T(128)}, ...), condition=%wide.region_12.13_spmd, body=%wide.region_5.12_spmd.sunk | while | flops 1107725824 | bytes 34693848 | solution.py:115
  60.8 11.9 %conditional.2 = (bf16[1,1,64,1024]{3,2,1,0:T(8,128)(2,1)S(1)}) conditional(s32[]{:T(128)} %bitcast.62, () %tuple.42, (bf16[8,1,64,1024]{3,2,1,0:T(8,128)(2,1)}, s32[]{:T(128)}, s32[8]{0:T(128)S(1)}, bf16[2,4096,2,128]{3,1,2,0:T(8,128)(2,1)}, bf16[8,1,64,2,128]{4,2,3,1,0:T(8,128)(2,1)S(1)}) %tuple.43), branch_computations={%region_6.6_spmd, %region_7.11_spmd} | conditional | flops 1107725824 | bytes 34431048 | solution.py:109
  63.5 1.7 dynamic-slice_bitcast_fusion
  74.7 11.9 %conditional.2 = (bf16[1,1,64,1024]{3,2,1,0:T(8,128)(2,1)S(1)}) conditional(s32[]{:T(128)} %bitcast.62, () %tuple.42, (bf16[8,1,64,1024]{3,2,1,0:T(8,128)(2,1)}, s32[]{:T(128)}, s32[8]{0:T(128)S(1)}, bf16[2,4096,2,128]{3,1,2,0:T(8,128)(2,1)}, bf16[8,1,64,2,128]{4,2,3,1,0:T(8,128)(2,1)S(1)}) %tuple.43), branch_computations={%region_6.6_spmd, %region_7.11_spmd} | conditional | flops 1107725824 | bytes 34431048 | solution.py:109
  77.5 1.7 dynamic-slice_bitcast_fusion
  88.7 11.9 %conditional.2 = (bf16[1,1,64,1024]{3,2,1,0:T(8,128)(2,1)S(1)}) conditional(s32[]{:T(128)} %bitcast.62, () %tuple.42, (bf16[8,1,64,1024]{3,2,1,0:T(8,128)(2,1)}, s32[]{:T(128)}, s32[8]{0:T(128)S(1)}, bf16[2,4096,2,128]{3,1,2,0:T(8,128)(2,1)}, bf16[8,1,64,2,128]{4,2,3,1,0:T(8,128)(2,1)S(1)}) %tuple.43), branch_computations={%region_6.6_spmd, %region_7.11_spmd} | conditional | flops 1107725824 | bytes 34431048 | solution.py:109
  102.7 11.9 %conditional.2 = (bf16[1,1,64,1024]{3,2,1,0:T(8,128)(2,1)S(1)}) conditional(s32[]{:T(128)} %bitcast.62, () %tuple.42, (bf16[8,1,64,1024]{3,2,1,0:T(8,128)(2,1)}, s32[]{:T(128)}, s32[8]{0:T(128)S(1)}, bf16[2,4096,2,128]{3,1,2,0:T(8,128)(2,1)}, bf16[8,1,64,2,128]{4,2,3,1,0:T(8,128)(2,1)S(1)}) %tuple.43), branch_computations={%region_6.6_spmd, %region_7.11_spmd} | conditional | flops 1107725824 | bytes 34431048 | solution.py:109
  116.7 11.9 %conditional.2 = (bf16[1,1,64,1024]{3,2,1,0:T(8,128)(2,1)S(1)}) conditional(s32[]{:T(128)} %bitcast.62, () %tuple.42, (bf16[8,1,64,1024]{3,2,1,0:T(8,128)(2,1)}, s32[]{:T(128)}, s32[8]{0:T(128)S(1)}, bf16[2,4096,2,128]{3,1,2,0:T(8,128)(2,1)}, bf16[8,1,64,2,128]{4,2,3,1,0:T(8,128)(2,1)S(1)}) %tuple.43), branch_computations={%region_6.6_spmd, %region_7.11_spmd} | conditional | flops 1107725824 | bytes 34431048 | solution.py:109
  130.7 11.9 %conditional.2 = (bf16[1,1,64,1024]{3,2,1,0:T(8,128)(2,1)S(1)}) conditional(s32[]{:T(128)} %bitcast.62, () %tuple.42, (bf16[8,1,64,1024]{3,2,1,0:T(8,128)(2,1)}, s32[]{:T(128)}, s32[8]{0:T(128)S(1)}, bf16[2,4096,2,128]{3,1,2,0:T(8,128)(2,1)}, bf16[8,1,64,2,128]{4,2,3,1,0:T(8,128)(2,1)S(1)}) %tuple.43), branch_computations={%region_6.6_spmd, %region_7.11_spmd} | conditional | flops 1107725824 | bytes 34431048 | solution.py:109
  144.6 11.9 %conditional.2 = (bf16[1,1,64,1024]{3,2,1,0:T(8,128)(2,1)S(1)}) conditional(s32[]{:T(128)} %bitcast.62, () %tuple.42, (bf16[8,1,64,1024]{3,2,1,0:T(8,128)(2,1)}, s32[]{:T(128)}, s32[8]{0:T(128)S(1)}, bf16[2,4096,2,128]{3,1,2,0:T(8,128)(2,1)}, bf16[8,1,64,2,128]{4,2,3,1,0:T(8,128)(2,1)S(1)}) %tuple.43), branch_computations={%region_6.6_spmd, %region_7.11_spmd} | conditional | flops 1107725824 | bytes 34431048 | solution.py:109
  158.6 11.9 %conditional.2 = (bf16[1,1,64,1024]{3,2,1,0:T(8,128)(2,1)S(1)}) conditional(s32[]{:T(128)} %bitcast.62, () %tuple.42, (bf16[8,1,64,1024]{3,2,1,0:T(8,128)(2,1)}, s32[]{:T(128)}, s32[8]{0:T(128)S(1)}, bf16[2,4096,2,128]{3,1,2,0:T(8,128)(2,1)}, bf16[8,1,64,2,128]{4,2,3,1,0:T(8,128)(2,1)S(1)}) %tuple.43), branch_computations={%region_6.6_spmd, %region_7.11_spmd} | conditional | flops 1107725824 | bytes 34431048 | solution.py:109
  171.2 3.5 %all-to-all-start.3 = ((bf16[4,128,1024]{2,1,0:T(8,128)(2,1)}), bf16[4,128,1024]{2,1,0:T(8,128)(2,1)S(1)}, u32[]{:S(2)}, u32[]{:S(2)}) async-start(bf16[4,128,1024]{2,1,0:T(8,128)(2,1)} %bitcast.69), calls=%async_computation.3 | async-start | bytes 2097152 | tf_op jit(solution)/shard_map/all_to_all | solution.py:116
  175.0 24.7 %all-to-all-done.3 = bf16[4,128,1024]{2,1,0:T(8,128)(2,1)S(1)} async-done(((bf16[4,128,1024]{2,1,0:T(8,128)(2,1)}), bf16[4,128,1024]{2,1,0:T(8,128)(2,1)S(1)}, u32[]{:S(2)}, u32[]{:S(2)}) %all-to-all-start.3) | async-done | bytes 1048608 | tf_op jit(solution)/shard_map/all_to_all | solution.py:116
  200.5 15.6 %convolution_bitcast_fusion = f32[8192,512]{0,1:T(8,128)} fusion(bf16[512,1024]{1,0:T(8,128)(2,1)S(1)} %bitcast_select_fusion, bf16[1024,8192]{1,0:T(8,128)(2,1)} %param.17), kind=kOutput, calls=%fused_computation.30 | convolution fusion | flops 8589934592 | bytes 34603008 | tf_op jit(solution)/shard_map/dot_general | solution.py:129
  216.2 124.2 %reduce-scatter.2.cloned.1.call-done = f32[2048,512]{0,1:T(8,128)} async-done(((f32[8192,512]{0,1:T(8,128)}), f32[2048,512]{0,1:T(8,128)}) %reduce-scatter.2.cloned.1.call-update) | async-done | bytes 4194320 | tf_op jit(solution)/shard_map/reduce_scatter | solution.py:128
  340.4 3.8 %convert_bitcast_fusion = bf16[512,2048]{1,0:T(8,128)(2,1)} fusion(f32[2048,512]{0,1:T(8,128)} %reduce-scatter.2.cloned.1.call-done), kind=kLoop, calls=%fused_computation.31 | loop fusion | flops 1048576 | bytes 6291456 | tf_op jit(solution)/shard_map/convert_element_type | solution.py:136
  (211 shorter events, 92.4 us)
Async XLA Ops:
  8.8 11.8 %all-to-all-start = ((bf16[4,1,2]{2,1,0:T(2,128)(2,1)}), bf16[4,1,2]{2,1,0:T(2,128)(2,1)S(1)}, u32[]{:S(2)}, u32[]{:S(2)}) async-start(bf16[4,1,2]{2,1,0:T(2,128)(2,1)} %all_to_all.20), calls=%async_computation | async-start | bytes 4096 | tf_op jit(solution)/shard_map/all_to_all | solution.py:92
  20.6 11.5 %all-to-all-start.2 = ((bf16[4,128,2,128]{3,1,2,0:T(8,128)(2,1)}), bf16[4,128,2,128]{3,1,2,0:T(8,128)(2,1)S(1)}, u32[]{:S(2)}, u32[]{:S(2)}) async-start(bf16[4,128,2,128]{3,1,2,0:T(8,128)(2,1)} %copy.35), calls=%async_computation.2 | async-start | bytes 524288 | tf_op jit(solution)/shard_map/all_to_all | solution.py:85
  32.1 27.3 %all-to-all-start.1 = ((bf16[4,128,1024]{2,1,0:T(8,128)(2,1)}), bf16[4,128,1024]{2,1,0:T(8,128)(2,1)}, u32[]{:S(2)}, u32[]{:S(2)}) async-start(bf16[4,128,1024]{2,1,0:T(8,128)(2,1)} %bitcast.17), calls=%async_computation.1 | async-start | bytes 2097152 | tf_op jit(solution)/shard_map/all_to_all | solution.py:78
  59.4 115.4 %copy-start = (s32[1,8]{1,0:T(1,128)S(1)}, s32[1,8]{1,0:T(1,128)}, u32[]{:S(2)}) copy-start(s32[1,8]{1,0:T(1,128)} %param.16) | copy-start | bytes 100
  171.2 28.5 %all-to-all-start.3 = ((bf16[4,128,1024]{2,1,0:T(8,128)(2,1)}), bf16[4,128,1024]{2,1,0:T(8,128)(2,1)S(1)}, u32[]{:S(2)}, u32[]{:S(2)}) async-start(bf16[4,128,1024]{2,1,0:T(8,128)(2,1)} %bitcast.69), calls=%async_computation.3 | async-start | bytes 2097152 | tf_op jit(solution)/shard_map/all_to_all | solution.py:116
  174.8 165.6 %reduce-scatter.2.cloned.1.call-start = ((), (), s32[]{:S(2)}) async-start(), calls=%async_computation.5 | async-start | bytes 20971520 | tf_op jit(solution)/shard_map/reduce_scatter | solution.py:128
Sparse Core Ops, SparseCore 0:
  216.3 124.0 reduce-scatter.1
where the time goes:
time: 352 us; the launch traced here: 351 us
  waiting for transfers between devices  174 us (49%)
  local copies, waits for them, and re-layouts  61.8 us (18%)
  matrix products  42.3 us (12%)
  loops' own time  23.2 us (7%)
  other arithmetic  19.2 us (5%)
  starting transfers between devices  17.5 us (5%)
  between operations  13.5 us (4%)
    reduce_scatter x1, waiting for transfers between devices, on_device(): lax.psum_scatter(lax.dot_general(out_weight, attended, (((0,), (1,)), (()...  124 us
    all_to_all x1, waiting for transfers between devices, on_device(): lax.all_to_all(results.reshape(replicas, capacity * qlength, width), 'rep...  24.7 us
    all_to_all x1, waiting for transfers between devices, on_device(): lax.all_to_all(send_query.reshape(replicas, capacity * qlength, width), '...  18.2 us
    dynamic_slice x24, local copies, waits for them, and re-layouts, on_device(): results = lax.map(run_question, (query_rows, own_rows, busy_rows, slot_of))  18 us
    another operation x8, loops' own time, run_question(): lax.cond(busy, lambda: attend_block(query_block, own_block, cache_slot),...  17.6 us
    dot_general x1, matrix products, on_device(): lax.dot_general(out_weight, attended, (((0,), (1,)), ((), ())), preferred...  15.6 us
    squeeze x8, local copies, waits for them, and re-layouts, run_question(): lax.dynamic_index_in_dim(cache_kv, slot_index, 0, keepdims=False)  13.9 us
    reduce_sum x16, other arithmetic, attend_block(): total = jnp.sum(far_exp, axis=-1) + jnp.sum(near_exp, axis=-1)  13.8 us
  transfers between devices with their start and end apart: 5, of which 5 were waited for; matrix products, arithmetic and copies ran while one was open for 3% of the time, Pallas kernels for 0%

commit v1 on v0

v1 whole, which is shorter than its diff:
```python
import functools
import math

import jax
import jax.numpy as jnp
from jax import lax
from jax.experimental import pallas as pl
from jax.experimental.pallas import tpu as pltpu
from jax.sharding import PartitionSpec as P

CAP = 2
BF16 = jnp.bfloat16
F32 = jnp.float32
LOG2E = 1.4426950408889634
TOTAL_MAX = 1e30


def pack_kernel(stored_ref, ids_ref, q_ref, own_ref, table_ref, *out_refs, questions, heads, qlength):
    replicas = len(out_refs)
    head_size = own_ref.shape[1]
    me = lax.axis_index("replica")
    for s, out_ref in enumerate(out_refs):
        haystack = stored_ref[lax.rem(me + s, replicas), 0]
        count = jnp.int32(0)
        found = [jnp.int32(-1)] * CAP
        for i in range(questions):
            hit = ids_ref[i, 0] == haystack
            for j in range(CAP):
                found[j] = jnp.where(hit & (count == j), jnp.int32(i), found[j])
            count = count + hit.astype(jnp.int32)
        for j in range(CAP):
            table_ref[s * CAP + j] = found[j]
            place = jnp.maximum(found[j], 0)
            rows = q_ref[pl.ds(pl.multiple_of(place * qlength, qlength), qlength), :]
            for h in range(heads):
                out_ref[j, h * qlength : (h + 1) * qlength, :] = rows[:, h * head_size : (h + 1) * head_size]
            own = own_ref[pl.ds(pl.multiple_of(place * 2 * qlength, 2 * qlength), 2 * qlength), :]
            out_ref[j, heads * qlength :, :] = own


def pack(stored, ids, queries, own, replicas):
    questions = ids.shape[0]
    head_size = own.shape[1]
    qlength = queries.shape[0] // questions
    heads = queries.shape[1] // head_size
    rows = heads * qlength + 2 * qlength
    smem = pl.BlockSpec(memory_space=pltpu.SMEM)
    vmem = pl.BlockSpec(memory_space=pltpu.VMEM)
    out = pl.pallas_call(
        functools.partial(pack_kernel, questions=questions, heads=heads, qlength=qlength),
        in_specs=[smem, smem, vmem, vmem],
        out_specs=[smem] + [vmem] * replicas,
        out_shape=[jax.ShapeDtypeStruct((replicas * CAP,), jnp.int32)]
        + [jax.ShapeDtypeStruct((CAP, rows, head_size), BF16)] * replicas,
        cost_estimate=pl.CostEstimate(flops=0, bytes_accessed=4 << 20, transcendentals=0),
        name="pack",
    )(stored, ids, queries, own)
    return out[0], out[1:]


def attend_kernel(x_ref, k_ref, vt_ref, o_ref, *, heads, qlength):
    context, head_size = k_ref.shape
    scale = LOG2E / math.sqrt(head_size)
    rows = heads * qlength
    qt = x_ref[0, :rows, :].T
    own = x_ref[0, rows:, :]
    near = jnp.dot(own, qt, preferred_element_type=F32) * scale
    u2 = lax.broadcasted_iota(jnp.int32, near.shape, 0)
    t = lax.broadcasted_iota(jnp.int32, near.shape, 1) % qlength
    valid = (u2 % 2 == 0) & (u2 <= 2 * t)
    near = jnp.where(valid, near, -jnp.inf)
    near_top = jnp.max(near, axis=0, keepdims=True)
    own_t = own.astype(F32).T.astype(BF16)
    ones = jnp.ones((16, context), BF16)
    vt = jnp.concatenate([vt_ref[...], ones], axis=0)
    own_vt = jnp.concatenate([own_t, ones[:, : 2 * qlength]], axis=0)

    def mix(top, far_weights):
        near_weights = pltpu.roll(jnp.exp2(near - top), 1, 0).astype(BF16)
        mixed = jnp.dot(vt, far_weights, preferred_element_type=F32)
        return mixed + jnp.dot(own_vt, near_weights, preferred_element_type=F32)

    def store(mixed):
        result = (mixed[:head_size] / mixed[head_size : head_size + 1]).T.astype(BF16)
        for h in range(heads):
            o_ref[:, h * head_size : (h + 1) * head_size] = result[h * qlength : (h + 1) * qlength, :]

    def far_scores():
        return jnp.dot(k_ref[...], qt, preferred_element_type=F32) * scale

    mixed = mix(near_top, jnp.exp2(far_scores() - near_top).astype(BF16))
    store(mixed)
    total = jnp.max(mixed[head_size : head_size + 1])

    @pl.when(jnp.logical_not(total < TOTAL_MAX))
    def _():
        scores = far_scores()
        top = jnp.maximum(near_top, jnp.max(scores, axis=0, keepdims=True))
        store(mix(top, jnp.exp2(scores - top).astype(BF16)))


def attend(x, keys, values_t, heads, qlength):
    number, rows, head_size = x.shape
    context = keys.shape[0]
    width = heads * head_size
    return pl.pallas_call(
        functools.partial(attend_kernel, heads=heads, qlength=qlength),
        grid=(number,),
        in_specs=[
            pl.BlockSpec((1, rows, head_size), lambda i: (i, 0, 0)),
            pl.BlockSpec((context, head_size), lambda i: (0, 0)),
            pl.BlockSpec((head_size, context), lambda i: (0, 0)),
        ],
        out_specs=pl.BlockSpec((qlength, width), lambda i: (i, 0)),
        out_shape=jax.ShapeDtypeStruct((number * qlength, width), BF16),
        cost_estimate=pl.CostEstimate(
            flops=8 * number * qlength * heads * context * head_size,
            bytes_accessed=4 << 20,
            transcendentals=number * qlength * heads * context,
        ),
        name="attend",
    )(x, keys, values_t)


def project_kernel(me_ref, a_ref, w_ref, give_ref, keep_ref, *, tiles):
    product = jnp.dot(a_ref[...], w_ref[...], preferred_element_type=F32)

    @pl.when(pl.program_id(0) < tiles)
    def _():
        give_ref[...] = product.astype(give_ref.dtype)

    @pl.when(pl.program_id(0) >= tiles)
    def _():
        keep_ref[...] = product


def project(me, rows, weight, flip, shares, tile):
    number, depth = rows.shape
    columns = weight.shape[1] // shares
    tiles = columns // tile

    def weight_map(i, me_ref):
        block = me_ref[0] ^ flip ^ (i < tiles).astype(jnp.int32)
        return 0, block * tiles + lax.rem(i, tiles)

    return pl.pallas_call(
        functools.partial(project_kernel, tiles=tiles),
        grid_spec=pltpu.PrefetchScalarGridSpec(
            num_scalar_prefetch=1,
            grid=(2 * tiles,),
            in_specs=[
                pl.BlockSpec((number, depth), lambda i, me_ref: (0, 0)),
                pl.BlockSpec((depth, tile), weight_map),
            ],
            out_specs=[
                pl.BlockSpec((number, tile), lambda i, me_ref: (0, jnp.minimum(i, tiles - 1))),
                pl.BlockSpec((number, tile), lambda i, me_ref: (0, jnp.maximum(i - tiles, 0))),
            ],
        ),
        out_shape=[
            jax.ShapeDtypeStruct((number, columns), BF16),
            jax.ShapeDtypeStruct((number, columns), F32),
        ],
        cost_estimate=pl.CostEstimate(
            flops=4 * number * depth * columns, bytes_accessed=4 * depth * columns, transcendentals=0
        ),
        name="project",
    )(me, rows, weight)


def finish_kernel(table_ref, counts_ref, kept_ref, core_ref, far_ref, *refs, first):
    o_ref = refs[-1]
    place = table_ref[first + pl.program_id(0)]
    total = kept_ref[...] + core_ref[...].astype(F32) + far_ref[...].astype(F32)
    t = lax.broadcasted_iota(jnp.int32, total.shape, 0)
    o_ref[...] = jnp.where(t < counts_ref[0, place], total, 0.0).astype(o_ref.dtype)


def finish(table, counts, kept, from_core, from_far, first, previous, rows, qlength):
    number, columns = kept.shape
    block = pl.BlockSpec((qlength, columns), lambda i, table_ref, counts_ref: (i, 0))
    extra = [] if previous is None else [previous]
    return pl.pallas_call(
        functools.partial(finish_kernel, first=first),
        grid_spec=pltpu.PrefetchScalarGridSpec(
            num_scalar_prefetch=2,
            grid=(number // qlength,),
            in_specs=[block] * 3 + [pl.BlockSpec(memory_space=pl.ANY)] * len(extra),
            out_specs=pl.BlockSpec(
                (qlength, columns), lambda i, table_ref, counts_ref: (table_ref[first + i], 0)
            ),
        ),
        out_shape=jax.ShapeDtypeStruct((rows, columns), BF16),
        input_output_aliases={5: 0} if extra else {},
        cost_estimate=pl.CostEstimate(flops=0, bytes_accessed=10 * number * columns, transcendentals=0),
        name="finish",
    )(table, counts, kept, from_core, from_far, *extra)


def on_device(queries, new_kv, cache_kv, stored, haystack_ids, token_counts, out_weight):
    replicas = lax.axis_size("replica")
    shares = lax.axis_size("tensor")
    head_size = cache_kv.shape[-1]
    questions = haystack_ids.shape[0]
    rows = queries.shape[0]
    qlength = rows // questions
    heads = queries.shape[1] // head_size
    table, packed = pack(stored, haystack_ids, queries, new_kv.reshape(2 * rows, head_size), replicas)
    keys = cache_kv[0, :, 0]
    values_t = cache_kv[0, :, 1].T
    phases = sorted(range(replicas), key=lambda s: (min(s, replicas - s), s))
    arrived = {}
    for s in phases:
        arrived[s] = packed[s]
        if s:
            arrived[s] = lax.ppermute(packed[s], "replica", [(i, (i + s) % replicas) for i in range(replicas)])
    returned = {}
    for s in phases:
        result = attend(arrived[s], keys, values_t, heads, qlength)
        if s:
            result = lax.ppermute(result, "replica", [(i, (i - s) % replicas) for i in range(replicas)])
        returned[s] = result

    if shares == 4 and replicas * CAP == questions:
        me = lax.axis_index("tensor").astype(jnp.int32).reshape(1)
        other_core = [(i, i ^ 1) for i in range(shares)]
        other_chip = [(i, i ^ 2) for i in range(shares)]
        tile = 512
        out = None
        for s in phases:
            far_give, far_keep = project(me, returned[s], out_weight, 2, shares, tile)
            far_core = lax.ppermute(far_give, "tensor", other_core)
            near_give, near_keep = project(me, returned[s], out_weight, 0, shares, tile)
            near_core = lax.ppermute(near_give, "tensor", other_core)
            chip_sum = (far_keep + far_core.astype(F32)).astype(BF16)
            far = lax.ppermute(chip_sum, "tensor", other_chip)
            out = finish(table, token_counts, near_keep, near_core, far, s * CAP, out, rows, qlength)
        return out

    blocks = jnp.stack([returned[s].reshape(CAP, qlength, -1) for s in range(replicas)])
    blocks = blocks.reshape(replicas * CAP, qlength, -1)
    match = table[None, :] == jnp.arange(questions, dtype=jnp.int32)[:, None]
    position = jnp.argmax(match.astype(jnp.int32), axis=1)
    used = jnp.arange(qlength, dtype=jnp.int32)[None, :] < token_counts[0][:, None]
    attended = jnp.where(used[..., None], blocks[position], jnp.zeros((), BF16)).reshape(rows, -1)
    summed = lax.psum_scatter(
        lax.dot_general(out_weight, attended, (((0,), (1,)), ((), ())), preferred_element_type=F32),
        "tensor",
        scatter_dimension=0,
        tiled=True,
    )
    return summed.T.astype(BF16)


def solution(mesh):
    in_specs = (
        P(("groups", "replica"), "tensor"),
        P(("groups", "replica"), None, "tensor"),
        P(("groups", "replica"), None, None, "tensor"),
        P("groups", None),
        P(("groups", "replica"), None),
        P(("groups", "replica"), None),
        P("tensor", None),
    )
    out_specs = P(("groups", "replica"), "tensor")
    return jax.shard_map(
        on_device, mesh=mesh, in_specs=in_specs, out_specs=out_specs, check_vma=False
    )
```

time: 352 us -> 197 us (0.56)
  waiting for transfers between devices: 174 us -> 24.6 us
  Pallas kernels: 0 us -> 132 us
  local copies, waits for them, and re-layouts: 61.8 us -> 19.2 us
  matrix products: 42.3 us -> 0 us
  loops' own time: 23.2 us -> 0 us
  other arithmetic: 19.2 us -> 2.59 us
  between operations: 13.5 us -> 0.15 us
    pallas_call x0 -> x17, Pallas kernels: none -> 132 us  [the longest x8 64.9 us: project(): pl.pallas_call(functools.partial(project_kernel, tiles=tiles), grid_spec=...]
    reduce_scatter x1 -> x0, waiting for transfers between devices: 124 us -> none  [on_device(): lax.psum_scatter(lax.dot_general(out_weight, attended, (((0,), (1,)), (()...]
    all_to_all x4 -> x0, waiting for transfers between devices: 49.3 us -> none  [the longest x1 24.7 us: on_device(): lax.all_to_all(results.reshape(replicas, capacity * qlength, width), 'rep...]
    dot_general x33 -> x0, matrix products: 42.3 us -> none  [the longest x1 15.6 us: on_device(): lax.dot_general(out_weight, attended, (((0,), (1,)), ((), ())), preferred...]
    ppermute x0 -> x18, waiting for transfers between devices: none -> 24.6 us  [the longest x4 24.6 us: on_device(): far = lax.ppermute(chip_sum, 'tensor', other_chip)]
    another operation x9 -> x0, loops' own time: 23.2 us -> none  [the longest x8 17.6 us: run_question(): lax.cond(busy, lambda: attend_block(query_block, own_block, cache_slot),...]
    dynamic_slice x24 -> x0, local copies, waits for them, and re-layouts: 18 us -> none  [on_device(): results = lax.map(run_question, (query_rows, own_rows, busy_rows, slot_of))]
    all_to_all x4 -> x0, starting transfers between devices: 17.5 us -> none  [the longest x1 6.35 us: on_device(): lax.all_to_all(send_code.reshape(replicas, capacity), 'replica', split_ax...]
  transfers between devices with their start and end apart: 5 -> 18, of which waited for: 5 -> 3; matrix products, arithmetic and copies ran while one was open for 3% -> 8% of each run, Pallas kernels for 0% -> 65%
where the time goes in v1:
time: 197 us; the launch traced here: 195 us
  Pallas kernels  132 us (67%)
  waiting for transfers between devices  24.6 us (12%)
  local copies, waits for them, and re-layouts  19.2 us (10%)
  starting transfers between devices  16 us (8%)
  other arithmetic  2.59 us (1%)
    pallas_call x8, Pallas kernels, project(): pl.pallas_call(functools.partial(project_kernel, tiles=tiles), grid_spec=...  64.9 us
    pallas_call x4, Pallas kernels, attend(): pl.pallas_call(functools.partial(attend_kernel, heads=heads, qlength=qlen...  52.8 us
    ppermute x4, waiting for transfers between devices, on_device(): far = lax.ppermute(chip_sum, 'tensor', other_chip)  24.6 us
    unnamed x32, local copies, waits for them, and re-layouts  12.5 us
    pallas_call x4, Pallas kernels, finish(): pl.pallas_call(functools.partial(finish_kernel, first=first), grid_spec=p...  12 us
    slice x1, local copies, waits for them, and re-layouts, on_device(): values_t = cache_kv[0, :, 1].T  6.65 us
    ppermute x3, starting transfers between devices, on_device(): lax.ppermute(packed[s], 'replica', [(i, (i + s) % replicas) for i in rang...  6.14 us
    ppermute x4, starting transfers between devices, on_device(): far = lax.ppermute(chip_sum, 'tensor', other_chip)  4.32 us
  transfers between devices with their start and end apart: 18, of which 3 were waited for; matrix products, arithmetic and copies ran while one was open for 8% of the time, Pallas kernels for 65%

profile of v1, /device:TPU:0, one launch (start us, length us, event | category | flops | bytes accessed | tf_op | source)
XLA Modules:
  0.0 194.9 jit_solution(13728971098797819797)
XLA Ops:
  2.7 2.6 %pack.1 = (s32[8]{0:T(128)}, bf16[2,640,128]{2,1,0:T(8,128)(2,1)}, bf16[2,640,128]{2,1,0:T(8,128)(2,1)}, bf16[2,640,128]{2,1,0:T(8,128)(2,1)}, bf16[2,640,128]{2,1,0:T(8,128)(2,1)}) custom-call(s32[4,2]{1,0:T(4,128)} %copy.11.stored_ref, s32[8,1]{1,0:T(8,128)} %copy.12.ids_ref, bf16[512,1024]{1,0:T(8,128)(2,1)} %q_ref.1, bf16[1024,128]{1,0:T(8,128)(2,1)} %bitcast.16), custom_call_target="tpu_custom_call" | custom-call | bytes 4194304 | tf_op jit(solution)/shard_map/pack/pallas_call | solution.py:49
  5.3 3.1 %collective-permute-start.10 = (bf16[2,640,128]{2,1,0:T(8,128)(2,1)}, bf16[2,640,128]{2,1,0:T(8,128)(2,1)}, u32[]{:S(2)}, u32[]{:S(2)}) collective-permute-start(bf16[2,640,128]{2,1,0:T(8,128)(2,1)} %get-tuple-element.37), channel_id=1, source_target_pairs={{0,4},{4,8},{8,12},{12,0},{1,5},{5,9},{9,13},{13,1},{2,6},{6,10},{... | collective-permute-start | bytes 983048 | tf_op jit(solution)/shard_map/ppermute | solution.py:216
  8.4 6.7 %fusion = (bf16[1,4096,1,128]{3,2,1,0:T(2,128)(2,1)}, bf16[1,4096,1,128]{3,2,1,0:T(2,128)(2,1)S(1)}) fusion(bf16[2,4096,2,128]{3,2,1,0:T(2,128)(2,1)} %param.9), kind=kLoop, calls=%fused_computation.5 | loop fusion | bytes 4194304 | tf_op jit(solution)/shard_map/slice | solution.py:210
  15.0 5.4 %copy.16 = bf16[1,4096,1,128]{1,3,2,0:T(8,128)(2,1)} copy(bf16[1,4096,1,128]{3,2,1,0:T(2,128)(2,1)} %get-tuple-element.47) | data formatting | bytes 2097152
  21.5 13.2 %attend.7.a_ref = bf16[128,1024]{1,0:T(8,128)(2,1)} custom-call(bf16[2,640,128]{2,1,0:T(8,128)(2,1)} %get-tuple-element.42.x_ref, bf16[4096,128]{1,0:T(8,128)(2,1)} %bitcast.12, bf16[128,4096]{1,0:T(8,128)(2,1)} %bitcast.8), custom_call_target="tpu_custom_call" | custom-call | flops 4294967296 | bytes 4194304 | tf_op jit(solution)/shard_map/attend/pallas_call | solution.py:106
  34.7 8.1 %project.15 = (bf16[128,2048]{1,0:T(8,128)(2,1)}, f32[128,2048]{1,0:T(8,128)}) custom-call(s32[1]{0:T(128)} %bitcast.1.me_ref, bf16[128,1024]{1,0:T(8,128)(2,1)} %attend.7.a_ref, bf16[1024,8192]{1,0:T(8,128)(2,1)} %w_ref.15), custom_call_target="tpu_custom_call" | custom-call | flops 1073741824 | bytes 8388608 | tf_op jit(solution)/shard_map/project/pallas_call | solution.py:146
  42.8 8.2 %project.14 = (bf16[128,2048]{1,0:T(8,128)(2,1)}, f32[128,2048]{1,0:T(8,128)}) custom-call(s32[1]{0:T(128)} %bitcast.1.me_ref, bf16[128,1024]{1,0:T(8,128)(2,1)} %attend.7.a_ref, bf16[1024,8192]{1,0:T(8,128)(2,1)} %w_ref.15), custom_call_target="tpu_custom_call" | custom-call | flops 1073741824 | bytes 8388608 | tf_op jit(solution)/shard_map/project/pallas_call | solution.py:146
  51.4 2.0 %collective-permute-start.5 = (bf16[2,640,128]{2,1,0:T(8,128)(2,1)S(1)}, bf16[2,640,128]{2,1,0:T(8,128)(2,1)S(1)}, u32[]{:S(2)}, u32[]{:S(2)}) collective-permute-start(bf16[2,640,128]{2,1,0:T(8,128)(2,1)S(1)} %copy-done.11), channel_id=1, source_target_pairs={{0,12},{4,0},{8,4},{12,8},{1,13},{5,1},{9,5},{13,9},{2,14},{6,2},{... | collective-permute-start | bytes 983048 | tf_op jit(solution)/shard_map/ppermute | solution.py:216
  54.5 13.2 %attend.6 = bf16[128,1024]{1,0:T(8,128)(2,1)} custom-call(bf16[2,640,128]{2,1,0:T(8,128)(2,1)} %collective-permute-done.10.x_ref, bf16[4096,128]{1,0:T(8,128)(2,1)} %bitcast.13, bf16[128,4096]{1,0:T(8,128)(2,1)} %bitcast.9), custom_call_target="tpu_custom_call" | custom-call | flops 4294967296 | bytes 4194304 | tf_op jit(solution)/shard_map/attend/pallas_call | solution.py:106
  69.7 13.2 %attend.5 = bf16[128,1024]{1,0:T(8,128)(2,1)} custom-call(bf16[2,640,128]{2,1,0:T(8,128)(2,1)} %copy-done.13, bf16[4096,128]{1,0:T(8,128)(2,1)} %bitcast.14, bf16[128,4096]{1,0:T(8,128)(2,1)} %bitcast.10), custom_call_target="tpu_custom_call" | custom-call | flops 4294967296 | bytes 4194304 | tf_op jit(solution)/shard_map/attend/pallas_call | solution.py:106
  84.3 13.2 %attend.4 = bf16[128,1024]{1,0:T(8,128)(2,1)} custom-call(bf16[2,640,128]{2,1,0:T(8,128)(2,1)} %copy-done.12, bf16[4096,128]{1,0:T(8,128)(2,1)} %bitcast.15, bf16[128,4096]{1,0:T(8,128)(2,1)} %bitcast.11), custom_call_target="tpu_custom_call" | custom-call | flops 4294967296 | bytes 4194304 | tf_op jit(solution)/shard_map/attend/pallas_call | solution.py:106
  100.2 8.1 %project.13 = (bf16[128,2048]{1,0:T(8,128)(2,1)}, f32[128,2048]{1,0:T(8,128)}) custom-call(s32[1]{0:T(128)} %bitcast.1.me_ref, bf16[128,1024]{1,0:T(8,128)(2,1)} %copy-done.2, bf16[1024,8192]{1,0:T(8,128)(2,1)} %w_ref.15), custom_call_target="tpu_custom_call" | custom-call | flops 1073741824 | bytes 8388608 | tf_op jit(solution)/shard_map/project/pallas_call | solution.py:146
  110.2 8.1 %project.12 = (bf16[128,2048]{1,0:T(8,128)(2,1)}, f32[128,2048]{1,0:T(8,128)}) custom-call(s32[1]{0:T(128)} %bitcast.1.me_ref, bf16[128,1024]{1,0:T(8,128)(2,1)} %copy-done.2, bf16[1024,8192]{1,0:T(8,128)(2,1)} %w_ref.15), custom_call_target="tpu_custom_call" | custom-call | flops 1073741824 | bytes 8388608 | tf_op jit(solution)/shard_map/project/pallas_call | solution.py:146
  119.0 8.1 %project.11 = (bf16[128,2048]{1,0:T(8,128)(2,1)}, f32[128,2048]{1,0:T(8,128)}) custom-call(s32[1]{0:T(128)} %bitcast.1.me_ref, bf16[128,1024]{1,0:T(8,128)(2,1)} %copy-done.1, bf16[1024,8192]{1,0:T(8,128)(2,1)} %w_ref.15), custom_call_target="tpu_custom_call" | custom-call | flops 1073741824 | bytes 8388608 | tf_op jit(solution)/shard_map/project/pallas_call | solution.py:146
  127.1 8.1 %project.10 = (bf16[128,2048]{1,0:T(8,128)(2,1)}, f32[128,2048]{1,0:T(8,128)}) custom-call(s32[1]{0:T(128)} %bitcast.1.me_ref, bf16[128,1024]{1,0:T(8,128)(2,1)} %copy-done.1, bf16[1024,8192]{1,0:T(8,128)(2,1)} %w_ref.15), custom_call_target="tpu_custom_call" | custom-call | flops 1073741824 | bytes 8388608 | tf_op jit(solution)/shard_map/project/pallas_call | solution.py:146
  135.9 8.0 %project.9 = (bf16[128,2048]{1,0:T(8,128)(2,1)}, f32[128,2048]{1,0:T(8,128)}) custom-call(s32[1]{0:T(128)} %bitcast.1.me_ref, bf16[128,1024]{1,0:T(8,128)(2,1)} %copy-done, bf16[1024,8192]{1,0:T(8,128)(2,1)} %w_ref.15), custom_call_target="tpu_custom_call" | custom-call | flops 1073741824 | bytes 8388608 | tf_op jit(solution)/shard_map/project/pallas_call | solution.py:146
  143.9 8.2 %project.8 = (bf16[128,2048]{1,0:T(8,128)(2,1)}, f32[128,2048]{1,0:T(8,128)}) custom-call(s32[1]{0:T(128)} %bitcast.1.me_ref, bf16[128,1024]{1,0:T(8,128)(2,1)} %copy-done, bf16[1024,8192]{1,0:T(8,128)(2,1)} %w_ref.15), custom_call_target="tpu_custom_call" | custom-call | flops 1073741824 | bytes 8388608 | tf_op jit(solution)/shard_map/project/pallas_call | solution.py:146
  158.3 3.0 %finish.4.refs_0_ = bf16[512,2048]{1,0:T(8,128)(2,1)} custom-call(s32[8]{0:T(128)} %get-tuple-element.26.table_ref, s32[1,8]{1,0:T(1,128)} %counts_ref.7, f32[128,2048]{1,0:T(8,128)} %get-tuple-element.43.kept_ref, bf16[128,2048]{1,0:T(8,128)(2,1)} %copy-done.7, bf16[128,2048]{1,0:T(8,128)(2,1)} %copy-done.8), custom_call_target="tpu_custom_call" | custom-call | bytes 2621440 | tf_op jit(solution)/shard_map/finish/pallas_call | solution.py:183
  161.3 8.9 %collective-permute-done.14.far_ref = bf16[128,2048]{1,0:T(8,128)(2,1)} collective-permute-done((bf16[128,2048]{1,0:T(8,128)(2,1)S(1)}, bf16[128,2048]{1,0:T(8,128)(2,1)}, u32[]{:S(2)}, u32[]{:S(2)}) %collective-permute-start.14) | collective-permute-done | bytes 524320 | tf_op jit(solution)/shard_map/ppermute | solution.py:236
  170.2 3.0 %finish.5.refs_0_ = bf16[512,2048]{1,0:T(8,128)(2,1)} custom-call(s32[8]{0:T(128)} %get-tuple-element.26.table_ref, s32[1,8]{1,0:T(1,128)} %counts_ref.7, f32[128,2048]{1,0:T(8,128)} %get-tuple-element.38.kept_ref, bf16[128,2048]{1,0:T(8,128)(2,1)} %collective-permute-done.12.core_ref, ...), custom_call_target="tpu_custom_call", output_to_operand_aliasing={{}: (5, {})} | custom-call | bytes 2621440 | tf_op jit(solution)/shard_map/finish/pallas_call | solution.py:183
  173.2 8.2 %collective-permute-done.9.far_ref = bf16[128,2048]{1,0:T(8,128)(2,1)} collective-permute-done((bf16[128,2048]{1,0:T(8,128)(2,1)S(1)}, bf16[128,2048]{1,0:T(8,128)(2,1)}, u32[]{:S(2)}, u32[]{:S(2)}) %collective-permute-start.9) | collective-permute-done | bytes 524320 | tf_op jit(solution)/shard_map/ppermute | solution.py:236
  181.4 3.0 %finish.6.refs_0_ = bf16[512,2048]{1,0:T(8,128)(2,1)} custom-call(s32[8]{0:T(128)} %get-tuple-element.26.table_ref, s32[1,8]{1,0:T(1,128)} %counts_ref.7, f32[128,2048]{1,0:T(8,128)} %get-tuple-element.33.kept_ref, bf16[128,2048]{1,0:T(8,128)(2,1)} %collective-permute-done.7.core_ref, ...), custom_call_target="tpu_custom_call", output_to_operand_aliasing={{}: (5, {})} | custom-call | bytes 2621440 | tf_op jit(solution)/shard_map/finish/pallas_call | solution.py:183
  184.4 7.5 %collective-permute-done.4.far_ref = bf16[128,2048]{1,0:T(8,128)(2,1)} collective-permute-done((bf16[128,2048]{1,0:T(8,128)(2,1)S(1)}, bf16[128,2048]{1,0:T(8,128)(2,1)}, u32[]{:S(2)}, u32[]{:S(2)}) %collective-permute-start.4) | collective-permute-done | bytes 524320 | tf_op jit(solution)/shard_map/ppermute | solution.py:236
  191.9 3.0 %finish.7 = bf16[512,2048]{1,0:T(8,128)(2,1)} custom-call(s32[8]{0:T(128)} %get-tuple-element.26.table_ref, s32[1,8]{1,0:T(1,128)} %counts_ref.7, f32[128,2048]{1,0:T(8,128)} %get-tuple-element.28.kept_ref, bf16[128,2048]{1,0:T(8,128)(2,1)} %copy-done.9, bf16[128,2048]{1,0:T(8,128)(2,1)} %collective-permute-done.4.far_ref, ...), custom_call_target="tpu_custom_call", output_to_operand_aliasing={{}: (5, {})} | custom-call | bytes 2621440 | tf_op jit(solution)/shard_map/finish/pallas_call | solution.py:183
  (66 shorter events, 20.6 us)
Async XLA Ops:
  5.3 49.2 %collective-permute-start.10 = (bf16[2,640,128]{2,1,0:T(8,128)(2,1)}, bf16[2,640,128]{2,1,0:T(8,128)(2,1)}, u32[]{:S(2)}, u32[]{:S(2)}) collective-permute-start(bf16[2,640,128]{2,1,0:T(8,128)(2,1)} %get-tuple-element.37), channel_id=1, source_target_pairs={{0,4},{4,8},{8,12},{12,0},{1,5},{5,9},{9,13},{13,1},{2,6},{6,10},{... | collective-permute-start | bytes 983048 | tf_op jit(solution)/shard_map/ppermute | solution.py:216
  42.8 8.6 %copy-start.11 = (bf16[2,640,128]{2,1,0:T(8,128)(2,1)S(1)}, bf16[2,640,128]{2,1,0:T(8,128)(2,1)}, u32[]{:S(2)}) copy-start(bf16[2,640,128]{2,1,0:T(8,128)(2,1)} %get-tuple-element.32) | copy-start | bytes 983044
  42.8 10.7 %copy-start.10 = (bf16[2,640,128]{2,1,0:T(8,128)(2,1)S(1)}, bf16[2,640,128]{2,1,0:T(8,128)(2,1)}, u32[]{:S(2)}) copy-start(bf16[2,640,128]{2,1,0:T(8,128)(2,1)} %get-tuple-element.27) | copy-start | bytes 983044
  42.8 65.5 %collective-permute-start.16 = (bf16[128,2048]{1,0:T(8,128)(2,1)}, bf16[128,2048]{1,0:T(8,128)(2,1)S(1)}, u32[]{:S(2)}, u32[]{:S(2)}) collective-permute-start(bf16[128,2048]{1,0:T(8,128)(2,1)} %get-tuple-element.46), channel_id=1, source_target_pairs={{0,1},{1,0},{2,3},{3,2},{4,5},{5,4},{6,7},{7,6},{8,9},{9,8},{10,11... | collective-permute-start | bytes 1572872 | tf_op jit(solution)/shard_map/ppermute | solution.py:232
  51.1 104.6 %collective-permute-start.15 = (bf16[128,2048]{1,0:T(8,128)(2,1)}, bf16[128,2048]{1,0:T(8,128)(2,1)S(1)}, u32[]{:S(2)}, u32[]{:S(2)}) collective-permute-start(bf16[128,2048]{1,0:T(8,128)(2,1)} %get-tuple-element.44), channel_id=1, source_target_pairs={{0,1},{1,0},{2,3},{3,2},{4,5},{5,4},{6,7},{7,6},{8,9},{9,8},{10,11... | collective-permute-start | bytes 1572872 | tf_op jit(solution)/shard_map/ppermute | solution.py:234
  51.4 17.6 %collective-permute-start.5 = (bf16[2,640,128]{2,1,0:T(8,128)(2,1)S(1)}, bf16[2,640,128]{2,1,0:T(8,128)(2,1)S(1)}, u32[]{:S(2)}, u32[]{:S(2)}) collective-permute-start(bf16[2,640,128]{2,1,0:T(8,128)(2,1)S(1)} %copy-done.11), channel_id=1, source_target_pairs={{0,12},{4,0},{8,4},{12,8},{1,13},{5,1},{9,5},{13,9},{2,14},{6,2},{... | collective-permute-start | bytes 983048 | tf_op jit(solution)/shard_map/ppermute | solution.py:216
  53.5 30.2 %collective-permute-start = (bf16[2,640,128]{2,1,0:T(8,128)(2,1)S(1)}, bf16[2,640,128]{2,1,0:T(8,128)(2,1)S(1)}, u32[]{:S(2)}, u32[]{:S(2)}) collective-permute-start(bf16[2,640,128]{2,1,0:T(8,128)(2,1)S(1)} %copy-done.10), channel_id=1, source_target_pairs={{0,8},{4,12},{8,0},{12,4},{1,9},{5,13},{9,1},{13,5},{2,10},{6,14},... | collective-permute-start | bytes 983048 | tf_op jit(solution)/shard_map/ppermute | solution.py:216
  67.7 31.8 %collective-permute-start.11 = (bf16[128,1024]{1,0:T(8,128)(2,1)}, bf16[128,1024]{1,0:T(8,128)(2,1)S(1)}, u32[]{:S(2)}, u32[]{:S(2)}) collective-permute-start(bf16[128,1024]{1,0:T(8,128)(2,1)} %attend.6), channel_id=1, source_target_pairs={{0,12},{4,0},{8,4},{12,8},{1,13},{5,1},{9,5},{13,9},{2,14},{6,2},{... | collective-permute-start | bytes 786440 | tf_op jit(solution)/shard_map/ppermute | solution.py:221
  82.9 35.4 %collective-permute-start.6 = (bf16[128,1024]{1,0:T(8,128)(2,1)}, bf16[128,1024]{1,0:T(8,128)(2,1)S(1)}, u32[]{:S(2)}, u32[]{:S(2)}) collective-permute-start(bf16[128,1024]{1,0:T(8,128)(2,1)} %attend.5), channel_id=1, source_target_pairs={{0,4},{4,8},{8,12},{12,0},{1,5},{5,9},{9,13},{13,1},{2,6},{6,10},{... | collective-permute-start | bytes 786440 | tf_op jit(solution)/shard_map/ppermute | solution.py:221
  97.6 10.7 %copy-start.3 = (f32[128,2048]{1,0:T(8,128)S(1)}, f32[128,2048]{1,0:T(8,128)}, u32[]{:S(2)}) copy-start(f32[128,2048]{1,0:T(8,128)} %get-tuple-element.45) | copy-start | bytes 3145732
  97.6 37.6 %collective-permute-start.1 = (bf16[128,1024]{1,0:T(8,128)(2,1)}, bf16[128,1024]{1,0:T(8,128)(2,1)S(1)}, u32[]{:S(2)}, u32[]{:S(2)}) collective-permute-start(bf16[128,1024]{1,0:T(8,128)(2,1)} %attend.4), channel_id=1, source_target_pairs={{0,8},{4,12},{8,0},{12,4},{1,9},{5,13},{9,1},{13,5},{2,10},{6,14},... | collective-permute-start | bytes 786440 | tf_op jit(solution)/shard_map/ppermute | solution.py:221
  108.3 43.9 %collective-permute-start.13 = (bf16[128,2048]{1,0:T(8,128)(2,1)}, bf16[128,2048]{1,0:T(8,128)(2,1)}, u32[]{:S(2)}, u32[]{:S(2)}) collective-permute-start(bf16[128,2048]{1,0:T(8,128)(2,1)} %get-tuple-element.41), channel_id=1, source_target_pairs={{0,1},{1,0},{2,3},{3,2},{4,5},{5,4},{6,7},{7,6},{8,9},{9,8},{10,11... | collective-permute-start | bytes 1572872 | tf_op jit(solution)/shard_map/ppermute | solution.py:232
  108.4 49.1 %collective-permute-start.17 = (bf16[128,2048]{1,0:T(8,128)(2,1)S(1)}, bf16[128,2048]{1,0:T(8,128)(2,1)S(1)}, u32[]{:S(2)}, u32[]{:S(2)}) collective-permute-start(bf16[128,2048]{1,0:T(8,128)(2,1)S(1)} %add_convert_fusion), channel_id=1, source_target_pairs={{0,2},{1,3},{2,0},{3,1},{4,6},{5,7},{6,4},{7,5},{8,10},{9,11},{10,... | collective-permute-start | bytes 1572872 | tf_op jit(solution)/shard_map/ppermute | solution.py:236
  118.3 39.2 %collective-permute-start.12 = (bf16[128,2048]{1,0:T(8,128)(2,1)}, bf16[128,2048]{1,0:T(8,128)(2,1)}, u32[]{:S(2)}, u32[]{:S(2)}) collective-permute-start(bf16[128,2048]{1,0:T(8,128)(2,1)} %get-tuple-element.39), channel_id=1, source_target_pairs={{0,1},{1,0},{2,3},{3,2},{4,5},{5,4},{6,7},{7,6},{8,9},{9,8},{10,11... | collective-permute-start | bytes 1572872 | tf_op jit(solution)/shard_map/ppermute | solution.py:234
  135.2 18.5 %collective-permute-start.8 = (bf16[128,2048]{1,0:T(8,128)(2,1)}, bf16[128,2048]{1,0:T(8,128)(2,1)}, u32[]{:S(2)}, u32[]{:S(2)}) collective-permute-start(bf16[128,2048]{1,0:T(8,128)(2,1)} %get-tuple-element.36), channel_id=1, source_target_pairs={{0,1},{1,0},{2,3},{3,2},{4,5},{5,4},{6,7},{7,6},{8,9},{9,8},{10,11... | collective-permute-start | bytes 1572872 | tf_op jit(solution)/shard_map/ppermute | solution.py:232
  143.9 8.5 %copy-start.4 = (f32[128,2048]{1,0:T(8,128)S(1)}, f32[128,2048]{1,0:T(8,128)}, u32[]{:S(2)}) copy-start(f32[128,2048]{1,0:T(8,128)} %get-tuple-element.40) | copy-start | bytes 3145732
  152.1 3.1 %collective-permute-start.3 = (bf16[128,2048]{1,0:T(8,128)(2,1)}, bf16[128,2048]{1,0:T(8,128)(2,1)S(1)}, u32[]{:S(2)}, u32[]{:S(2)}) collective-permute-start(bf16[128,2048]{1,0:T(8,128)(2,1)} %get-tuple-element.31), channel_id=1, source_target_pairs={{0,1},{1,0},{2,3},{3,2},{4,5},{5,4},{6,7},{7,6},{8,9},{9,8},{10,11... | collective-permute-start | bytes 1572872 | tf_op jit(solution)/shard_map/ppermute | solution.py:232
  152.4 3.1 %copy-start.6 = (f32[128,2048]{1,0:T(8,128)S(1)}, f32[128,2048]{1,0:T(8,128)}, u32[]{:S(2)}) copy-start(f32[128,2048]{1,0:T(8,128)} %get-tuple-element.30) | copy-start | bytes 3145732
  153.7 19.5 %collective-permute-start.7 = (bf16[128,2048]{1,0:T(8,128)(2,1)}, bf16[128,2048]{1,0:T(8,128)(2,1)}, u32[]{:S(2)}, u32[]{:S(2)}) collective-permute-start(bf16[128,2048]{1,0:T(8,128)(2,1)} %get-tuple-element.34), channel_id=1, source_target_pairs={{0,1},{1,0},{2,3},{3,2},{4,5},{5,4},{6,7},{7,6},{8,9},{9,8},{10,11... | collective-permute-start | bytes 1572872 | tf_op jit(solution)/shard_map/ppermute | solution.py:234
  155.2 15.0 %collective-permute-start.14 = (bf16[128,2048]{1,0:T(8,128)(2,1)S(1)}, bf16[128,2048]{1,0:T(8,128)(2,1)}, u32[]{:S(2)}, u32[]{:S(2)}) collective-permute-start(bf16[128,2048]{1,0:T(8,128)(2,1)S(1)} %add_convert_fusion.1), channel_id=1, source_target_pairs={{0,2},{1,3},{2,0},{3,1},{4,6},{5,7},{6,4},{7,5},{8,10},{9,11},{10,... | collective-permute-start | bytes 1572872 | tf_op jit(solution)/shard_map/ppermute | solution.py:236
  155.7 25.7 %collective-permute-start.9 = (bf16[128,2048]{1,0:T(8,128)(2,1)S(1)}, bf16[128,2048]{1,0:T(8,128)(2,1)}, u32[]{:S(2)}, u32[]{:S(2)}) collective-permute-start(bf16[128,2048]{1,0:T(8,128)(2,1)S(1)} %add_convert_fusion.2), channel_id=1, source_target_pairs={{0,2},{1,3},{2,0},{3,1},{4,6},{5,7},{6,4},{7,5},{8,10},{9,11},{10,... | collective-permute-start | bytes 1572872 | tf_op jit(solution)/shard_map/ppermute | solution.py:236
  157.5 26.9 %collective-permute-start.2 = (bf16[128,2048]{1,0:T(8,128)(2,1)}, bf16[128,2048]{1,0:T(8,128)(2,1)S(1)}, u32[]{:S(2)}, u32[]{:S(2)}) collective-permute-start(bf16[128,2048]{1,0:T(8,128)(2,1)} %get-tuple-element.29), channel_id=1, source_target_pairs={{0,1},{1,0},{2,3},{3,2},{4,5},{5,4},{6,7},{7,6},{8,9},{9,8},{10,11... | collective-permute-start | bytes 1572872 | tf_op jit(solution)/shard_map/ppermute | solution.py:234
  157.5 34.4 %collective-permute-start.4 = (bf16[128,2048]{1,0:T(8,128)(2,1)S(1)}, bf16[128,2048]{1,0:T(8,128)(2,1)}, u32[]{:S(2)}, u32[]{:S(2)}) collective-permute-start(bf16[128,2048]{1,0:T(8,128)(2,1)S(1)} %add_convert_fusion.3), channel_id=1, source_target_pairs={{0,2},{1,3},{2,0},{3,1},{4,6},{5,7},{6,4},{7,5},{8,10},{9,11},{10,... | collective-permute-start | bytes 1572872 | tf_op jit(solution)/shard_map/ppermute | solution.py:236
  184.4 7.5 %copy-start.9 = (bf16[128,2048]{1,0:T(8,128)(2,1)}, bf16[128,2048]{1,0:T(8,128)(2,1)S(1)}, u32[]{:S(2)}) copy-start(bf16[128,2048]{1,0:T(8,128)(2,1)S(1)} %collective-permute-done.2.core_ref) | copy-start | bytes 1572868
  (8 other events, 8.4 us)
